TPU v7x, 32 devices: a whole 2x2x4 slice. The times are simulated.
32 devices in a mesh: clip: 2 (over x), space: 4 (over y, core), tm: 4 (over z).
Axes of the slice: x: 2, y: 2, z: 4, core: 2. Of those that a mesh axis runs over, the one named last changes fastest.
Arguments:
- block_input: bfloat16 [8, 12, 160, 384], P(('clip', 'tm'), 'space'), parts along dimension 0, may hold values from -24 to 24, as said below
- conv_input: bfloat16 [8, 12, 160, 384], P(('clip', 'tm'), 'space'), parts along dimension 0, may hold values from -24 to 24, as said below
- norm_gain: float32 [384], replicated, may hold values from 0.1 to 1.9
- norm_bias: float32 [384], replicated, may hold values from -3 to 3
- conv_weight: bfloat16 [3, 3, 3, 384, 384], replicated, may hold values from -0.0625 to 0.0625
- conv_bias: float32 [384], replicated, may hold values from -1.5 to 1.5
- attn_gain: float32 [384], replicated, may hold values from 0.1 to 1.9
- attn_bias: float32 [384], replicated, may hold values from -1.5 to 1.5
- query_weight: bfloat16 [384, 384], replicated, may hold values from -4 to 4
- query_bias: float32 [384], replicated, may hold values from -1.5 to 1.5
- key_weight: bfloat16 [384, 384], replicated, may hold values from -4 to 4
- value_weight: bfloat16 [384, 384], replicated, may hold values from -0.3125 to 0.3125
- value_bias: float32 [384], replicated, may hold values from -3 to 3
- out_weight: bfloat16 [384, 384], replicated, may hold values from -0.3125 to 0.3125
- out_bias: float32 [384], replicated, may hold values from -3 to 3
Outputs:
- block_output: bfloat16 [8, 12, 160, 384], P(('clip', 'tm'), 'space'), parts along dimension 0
There are 2 independent parts, one for each index of `clip`. A program takes and returns all parts, laid end to end along the dimension named above; an argument that names none is the same for every part. Nothing has to cross between parts.
Inputs may be any that keep to these rules, and one draw needn't show every extreme that they name: `block_input`: finite activations. `conv_input`: finite activations.
All inputs are finite; a program needn't handle non-finite values.
Results may differ from a plain program's by a relative error of at most 0.0075.
Values may be sent and summed in bfloat16 or wider, within the bound.
No kernel may reach another device: no remote copies, remote signals or barrier semaphores. Data moves between devices by JAX's collectives and lax.ppermute only.
A program may use at most 128 MiB of HBM per device.

v0:
```python
import jax
import jax.numpy as jnp
from jax import lax
from jax.sharding import PartitionSpec as P


def from_behind(value, axis, steps):
    count = lax.axis_size(axis)
    leading, last = (max(0, -steps), min(count, count - steps))
    return lax.ppermute(value, axis, [(source, source + steps) for source in range(leading, last)])


def padded_2(x, sides, width):
    for axis, dim in sides:
        peers, length = (lax.axis_size(axis), x.shape[dim])
        up = [(i, (i + 1) % peers) for i in range(peers - 1)]
        down = [(j, i) for i, j in up]
        last = lax.slice_in_dim(x, length - width, length, axis=dim)
        leading = lax.slice_in_dim(x, 0, width, axis=dim)
        before = lax.ppermute(last, axis, up)
        after = lax.ppermute(leading, axis, down)
        x = jnp.concatenate([before, x, after], axis=dim)
    return x


def rms_norm(field, gain, bias):
    mean_square = jnp.mean(field * field, axis=-1, keepdims=True)
    return field * lax.rsqrt(mean_square + 1e-06) * gain + bias


def causal_conv(padded, conv_weight, frame_count, row_count, columns):
    channels = padded.shape[-1]
    running = jnp.zeros((frame_count * row_count * columns, channels), jnp.float32)
    for tap_t in range(3):
        for tap_y in range(3):
            window = padded[tap_t : tap_t + frame_count, tap_y : tap_y + row_count]
            joined = jnp.concatenate(
                [window[:, :, tap_x : tap_x + columns] for tap_x in range(3)], axis=-1
            )
            joined = joined.reshape(-1, 3 * channels)
            kernel = conv_weight[tap_t, tap_y].reshape(3 * channels, channels)
            running = running + jnp.dot(joined, kernel, preferred_element_type=jnp.float32)
    return running.reshape(frame_count, row_count, columns, channels)


def absorb(state, queries, key_rows, value_rows, score_scale):
    numer_acc, denom_acc, max_acc = state
    scores = (
        jnp.einsum("fqc,fkc->fqk", queries, key_rows, preferred_element_type=jnp.float32)
        * score_scale
    )
    new_max = jnp.maximum(max_acc, jnp.max(scores, axis=-1))
    expd = jnp.exp(scores - new_max[..., None])
    weights = expd.astype(jnp.bfloat16)
    added = jnp.einsum("fqk,fkc->fqc", weights, value_rows, preferred_element_type=jnp.float32)
    numer_acc = added
    denom_acc = jnp.sum(expd, axis=-1)
    return (numer_acc, denom_acc, new_max)


def shards(
    block_input,
    conv_input,
    norm_gain,
    norm_bias,
    conv_weight,
    conv_bias,
    attn_gain,
    attn_bias,
    query_weight,
    query_bias,
    key_weight,
    value_weight,
    value_bias,
    out_weight,
    out_bias,
):
    frame_count, row_count, columns, channels = block_input.shape
    field = conv_input.astype(jnp.float32)
    activated = jax.nn.silu(rms_norm(field, norm_gain, norm_bias)).astype(jnp.bfloat16)
    earlier = [from_behind(activated, "tm", offset) for offset in (1, 2)]
    stacked = jnp.concatenate([earlier[1], earlier[0], activated], axis=0)
    padded = padded_2(stacked, (("space", 1),), 1)
    padded = jnp.pad(padded, ((0, 0), (0, 0), (1, 1), (0, 0)))
    convolved = causal_conv(padded, conv_weight, frame_count, row_count, columns) + conv_bias
    mixed = (block_input.astype(jnp.float32) + convolved).astype(jnp.bfloat16)
    mixed_wide = mixed.astype(jnp.float32)
    normed = rms_norm(mixed_wide, attn_gain, attn_bias).astype(jnp.bfloat16)
    flat_rows = normed.reshape(frame_count, row_count * columns, channels)
    score_scale = float(channels) ** (-0.5)
    queries = (
        jnp.dot(flat_rows, query_weight, preferred_element_type=jnp.float32) + query_bias
    ).astype(jnp.bfloat16)
    query_count = row_count * columns
    start_state = (
        jnp.zeros((frame_count, query_count, channels), jnp.float32),
        jnp.zeros((frame_count, query_count), jnp.float32),
        jnp.full((frame_count, query_count), -1e30, jnp.float32),
    )
    source = lax.all_gather(normed, "space", axis=1, tiled=True).reshape(frame_count, -1, channels)
    key_rows = jnp.dot(source, key_weight, preferred_element_type=jnp.float32).astype(jnp.bfloat16)
    value_rows = (
        jnp.dot(source, value_weight, preferred_element_type=jnp.float32) + value_bias
    ).astype(jnp.bfloat16)
    numer_acc, denom_acc, max_acc = absorb(start_state, queries, key_rows, value_rows, score_scale)
    attended = (numer_acc / denom_acc[..., None]).astype(jnp.bfloat16)
    projected = jnp.dot(attended, out_weight, preferred_element_type=jnp.float32) + out_bias
    return (mixed_wide + projected.reshape(mixed_wide.shape)).astype(jnp.bfloat16)


def solution(mesh):
    placed = (
        P(("clip", "tm"), "space", None, None),
        P(("clip", "tm"), "space", None, None),
        P(),
        P(),
        P(),
        P(),
        P(),
        P(),
        P(),
        P(),
        P(),
        P(),
        P(),
        P(),
        P(),
    )
    return jax.shard_map(
        shards,
        mesh=mesh,
        in_specs=placed,
        out_specs=P(("clip", "tm"), "space", None, None),
        check_vma=False,
    )
```

profile of v0, /device:TPU:0, one launch (start us, length us, event | category | flops | bytes accessed | tf_op | source)
XLA Modules:
  0.0 103.6 jit_solution(10755714841860632833)
XLA Ops:
  6.5 0.0 all-gather.2.cloned.1.call-start
  6.5 1.2 %fusion.35 = f32[3,160]{1,0:T(4,128)S(1)} fusion(bf16[1,3,160,384]{3,2,1,0:T(8,128)(2,1)} %param.16), kind=kLoop, calls=%fused_computation.72 | loop fusion | flops 552480 | bytes 370560 | tf_op jit(solution)/shard_map/reduce_sum | solution.py:27
  7.8 1.3 %fusion.43 = bf16[1,3,160,384]{3,2,1,0:T(8,128)(2,1)S(1)} fusion(bf16[1,3,160,384]{3,2,1,0:T(8,128)(2,1)} %param.16, f32[384]{0:T(512)} %param.18, f32[384]{0:T(512)} %param.17, f32[3,160]{1,0:T(4,128)S(1)} %add_rsqrt_fusion.1), kind=kLoop, calls=%fused_computation.80 | loop fusion | flops 1658880 | bytes 742272 | tf_op jit(solution)/shard_map/convert_element_type | solution.py:80
  9.1 5.0 %collective-permute-start.1 = (bf16[1,3,160,384]{3,2,1,0:T(8,128)(2,1)S(1)}, bf16[1,3,160,384]{3,2,1,0:T(8,128)(2,1)S(1)}, u32[]{:S(2)}, u32[]{:S(2)}) collective-permute-start(bf16[1,3,160,384]{3,2,1,0:T(8,128)(2,1)S(1)} %fusion.43), channel_id=1, source_target_pairs={{0,1},{1,2},{2,3},{4,5},{5,6},{6,7},{8,9},{9,10},{10,11},{12,13},{... | collective-permute-start | bytes 1105928 | tf_op jit(solution)/shard_map/ppermute | solution.py:10
  14.1 4.5 %collective-permute-start = (bf16[1,3,160,384]{3,2,1,0:T(8,128)(2,1)S(1)}, bf16[1,3,160,384]{3,2,1,0:T(8,128)(2,1)S(1)}, u32[]{:S(2)}, u32[]{:S(2)}) collective-permute-start(bf16[1,3,160,384]{3,2,1,0:T(8,128)(2,1)S(1)} %fusion.43), channel_id=1, source_target_pairs={{0,2},{1,3},{4,6},{5,7},{8,10},{9,11},{12,14},{13,15},{16,18},{17,... | collective-permute-start | bytes 1105928 | tf_op jit(solution)/shard_map/ppermute | solution.py:10
  18.6 4.4 %collective-permute-done.1 = bf16[1,3,160,384]{3,2,1,0:T(8,128)(2,1)S(1)} collective-permute-done((bf16[1,3,160,384]{3,2,1,0:T(8,128)(2,1)S(1)}, bf16[1,3,160,384]{3,2,1,0:T(8,128)(2,1)S(1)}, u32[]{:S(2)}, u32[]{:S(2)}) %collective-permute-start.1) | collective-permute-done | bytes 368672 | tf_op jit(solution)/shard_map/ppermute | solution.py:10
  23.0 6.8 %collective-permute-done = bf16[1,3,160,384]{3,2,1,0:T(8,128)(2,1)S(1)} collective-permute-done((bf16[1,3,160,384]{3,2,1,0:T(8,128)(2,1)S(1)}, bf16[1,3,160,384]{3,2,1,0:T(8,128)(2,1)S(1)}, u32[]{:S(2)}, u32[]{:S(2)}) %collective-permute-start) | collective-permute-done | bytes 368672 | tf_op jit(solution)/shard_map/ppermute | solution.py:10
  29.8 0.1 pad_maximum_fusion.21
  29.9 1.3 %collective-permute-start.2 = (bf16[3,1,160,384]{3,2,1,0:T(8,128)(2,1)S(1)}, bf16[3,1,160,384]{3,2,1,0:T(8,128)(2,1)S(1)}, u32[]{:S(2)}, u32[]{:S(2)}) collective-permute-start(bf16[3,1,160,384]{3,2,1,0:T(8,128)(2,1)S(1)} %get-tuple-element.41), channel_id=1, source_target_pairs={{0,4},{4,8},{8,12},{1,5},{5,9},{9,13},{2,6},{6,10},{10,14},{3,7},{... | collective-permute-start | bytes 1105928 | tf_op jit(solution)/shard_map/ppermute | solution.py:20
  31.3 1.3 %collective-permute-start.3 = (bf16[3,1,160,384]{3,2,1,0:T(8,128)(2,1)S(1)}, bf16[3,1,160,384]{3,2,1,0:T(8,128)(2,1)S(1)}, u32[]{:S(2)}, u32[]{:S(2)}) collective-permute-start(bf16[3,1,160,384]{3,2,1,0:T(8,128)(2,1)S(1)} %get-tuple-element.40), channel_id=1, source_target_pairs={{4,0},{8,4},{12,8},{5,1},{9,5},{13,9},{6,2},{10,6},{14,10},{7,3},{... | collective-permute-start | bytes 1105928 | tf_op jit(solution)/shard_map/ppermute | solution.py:21
  32.6 3.9 %fusion.53 = (bf16[1,1,3,384,384]{4,3,2,1,0:T(8,128)(2,1)S(1)}, bf16[1,1,3,384,384]{4,3,2,1,0:T(8,128)(2,1)S(1)}, bf16[1,1,3,384,384]{4,3,2,1,0:T(8,128)(2,1)S(1...) fusion(bf16[3,3,3,384,384]{4,3,2,1,0:T(8,128)(2,1)} %param.19), kind=kLoop, calls=%fused_computation.96 | loop fusion | bytes 15925248 | tf_op jit(solution)/shard_map/slice | solution.py:41
  36.5 0.0 collective-permute-done.2
  36.5 0.1 collective-permute-done.3
  36.6 1.5 %select_maximum_fusion = bf16[3,5,162,384]{3,2,1,0:T(8,128)(2,1)S(1)} fusion(bf16[3,1,160,384]{3,2,1,0:T(8,128)(2,1)S(1)} %collective-permute-done.3, bf16[3,1,160,384]{3,2,1,0:T(8,128)(2,1)S(1)} %collective-permute-done.2, bf16[1,3,160,384]{3,2,1,0:T(8,128)(2,1)S(1)} %fusion.43, bf16[1,3,160,384]{3,2,1,0:T(8,128)(2,1)S(1)} %collective-permute-done.1, ...), kind=kLoop, calls=%fused_computation.10 | loop fusion | flops 16796160 | bytes 3709440 | tf_op jit(solution)/shard_map/concatenate | solution.py:22
  38.1 1.1 %fusion.54 = (bf16[1,3,160,384]{3,2,1,0:T(8,128)(2,1)S(1)}, bf16[1,3,160,384]{3,2,1,0:T(8,128)(2,1)S(1)}, bf16[1,3,160,384]{3,2,1,0:T(8,128)(2,1)S(1)}, bf16[1,3...) fusion(bf16[3,5,162,384]{3,2,1,0:T(8,128)(2,1)S(1)} %select_max, ...), kind=kLoop, calls=%fused_computation.97 | loop fusion | bytes 13271040 | tf_op jit(solution)/shard_map/slice | solution.py:38
  39.3 1.3 %fusion.26 = (bf16[1,3,160,1152]{3,2,1,0:T(8,128)(2,1)S(1)}, bf16[1,3,160,1152]{3,2,1,0:T(8,128)(2,1)S(1)}, bf16[1,3,160,1152]{3,2,1,0:T(8,128)(2,1)S(1)}) fusion(bf16[3,1,160,384]{3,2,1,0:T(8,128)(2,1)S(1)} %collective-permute-done.2, bf16[1,3,160,384]{3,2,1,0:T(8,128)(2,1)S(1)} %fusion.43, bf16[1,3,160,384]{3,2,1,0:T(8,128)(2,1)S(1)} %collective-permute-done.1, ...), kind=kLoop, calls=%fused_computation.41 | loop fusion | flops 19906560 | bytes 7004160 | tf_op jit(solution)/shard_map/concatenate | solution.py:37
  40.5 0.8 fusion.55
  41.3 0.1 pad_maximum_fusion.20
  41.4 0.2 pad_maximum_fusion.18
  41.6 0.8 convolution_add_fusion.10
  42.4 0.5 fusion.24
  43.0 0.8 convolution_add_fusion.9
  43.7 0.8 convolution_add_fusion.8
  44.5 0.8 convolution_add_fusion.7
  45.3 0.8 convolution_add_fusion.6
  46.0 0.8 convolution_add_fusion.5
  46.8 0.8 convolution_add_fusion.4
  47.6 0.0 copy-start.2
  47.6 0.0 copy-start.3
  47.6 0.0 copy-start.4
  47.6 0.0 copy-start.5
  47.6 0.8 convolution_add_fusion.3
  48.4 0.0 copy-start.7
  48.4 0.0 copy-start.10
  48.4 0.1 copy-done.2
  48.6 0.2 fusion.44
  48.8 0.9 fusion.47
  49.7 0.0 all-gather.2.cloned.1.call-update
  49.8 0.0 copy-done.7
  49.8 1.4 %fusion.14 = bf16[480,384]{1,0:T(8,128)(2,1)S(1)} fusion(bf16[480,384]{1,0:T(8,128)(2,1)} %bitcast.75, bf16[384,384]{1,0:T(8,128)(2,1)S(1)} %copy-done.7, f32[384]{0:T(512)S(1)} %copy-done.10), kind=kOutput, calls=%fused_computation.31 | convolution fusion | flops 141926400 | bytes 1033728 | tf_op jit(solution)/shard_map/dot_general | solution.py:92
  51.2 32.2 %all-gather.2.cloned.1.call-done = bf16[1,12,160,384]{3,2,0,1:T(8,128)(2,1)} async-done(((bf16[1,3,160,384]{3,2,0,1:T(8,128)(2,1)}), bf16[1,12,160,384]{3,2,0,1:T(8,128)(2,1)}) %all-gather.2.cloned.1.call-update) | async-done | bytes 1474576 | tf_op jit(solution)/shard_map/all_gather | solution.py:100
  83.4 5.3 %multiply_reduce_fusion = (f32[480]{0:T(512)S(1)}, f32[480,1920]{1,0:T(8,128)}) fusion(bf16[480,384]{1,0:T(8,128)(2,1)S(1)} %fusion.14, bf16[1920,384]{1,0:T(8,128)(2,1)} %bitcast.79, bf16[384,384]{1,0:T(8,128)(2,1)S(1)} %copy-done), kind=kOutput, calls=%fused_computation.4 | convolution fusion | flops 1276599808 | bytes 5826432 | tf_op jit(solution)/shard_map/fqc,fkc->fqk/dot_general | solution.py:49
  88.7 2.2 %fusion.3 = bf16[1920,384]{1,0:T(8,128)(2,1)} fusion(bf16[1920,384]{1,0:T(8,128)(2,1)S(1)} %bitcast.80, bf16[384,384]{1,0:T(8,128)(2,1)S(1)} %copy-done.8, f32[384]{0:T(512)S(1)} %copy-done.11), kind=kOutput, calls=%fused_computation.9 | convolution fusion | flops 567705600 | bytes 3245568 | tf_op jit(solution)/shard_map/dot_general | solution.py:103
  90.9 0.7 fusion.1
  91.7 0.2 copy-done.9
  91.9 0.5 copy-done.13
  92.4 3.5 %convolution_add_fusion.1 = f32[480,384]{1,0:T(8,128)S(1)} fusion(bf16[384,384]{1,0:T(8,128)(2,1)S(1)} %copy-done.9, bf16[1920,384]{1,0:T(8,128)(2,1)S(1)} %copy-done.13, f32[480,1920]{1,0:T(8,128)} %get-tuple-element.43, f32[480]{0:T(512)S(1)} %broadcast_maximum_fusion, f32[384]{0:T(512)S(1)} %copy-done.12, f32[480]{0:T(512)S(1)} %fusion.1), kind=kOutput, calls=%fused_computation.21 | convolution fusion | flops 852664320 | bytes 6198528 | tf_op jit(solution)/shard_map/dot_general | solution.py:107
  96.0 0.8 fusion.49
  (21 shorter events, 0.1 us)
Async XLA Ops:
  6.5 76.8 %copy-start = (bf16[384,384]{1,0:T(8,128)(2,1)S(1)}, bf16[384,384]{1,0:T(8,128)(2,1)}, u32[]{:S(2)}) copy-start(bf16[384,384]{1,0:T(8,128)(2,1)} %param.25) | copy-start | bytes 884740
  6.5 76.8 %all-gather.2.cloned.1.call-start = ((), (), s32[]{:S(2)}) async-start(), calls=%async_computation | async-start | bytes 1843200 | tf_op jit(solution)/shard_map/all_gather | solution.py:100
  9.1 13.9 %collective-permute-start.1 = (bf16[1,3,160,384]{3,2,1,0:T(8,128)(2,1)S(1)}, bf16[1,3,160,384]{3,2,1,0:T(8,128)(2,1)S(1)}, u32[]{:S(2)}, u32[]{:S(2)}) collective-permute-start(bf16[1,3,160,384]{3,2,1,0:T(8,128)(2,1)S(1)} %fusion.43), channel_id=1, source_target_pairs={{0,1},{1,2},{2,3},{4,5},{5,6},{6,7},{8,9},{9,10},{10,11},{12,13},{... | collective-permute-start | bytes 1105928 | tf_op jit(solution)/shard_map/ppermute | solution.py:10
  14.1 15.8 %collective-permute-start = (bf16[1,3,160,384]{3,2,1,0:T(8,128)(2,1)S(1)}, bf16[1,3,160,384]{3,2,1,0:T(8,128)(2,1)S(1)}, u32[]{:S(2)}, u32[]{:S(2)}) collective-permute-start(bf16[1,3,160,384]{3,2,1,0:T(8,128)(2,1)S(1)} %fusion.43), channel_id=1, source_target_pairs={{0,2},{1,3},{4,6},{5,7},{8,10},{9,11},{12,14},{13,15},{16,18},{17,... | collective-permute-start | bytes 1105928 | tf_op jit(solution)/shard_map/ppermute | solution.py:10
  29.9 6.6 %collective-permute-start.2 = (bf16[3,1,160,384]{3,2,1,0:T(8,128)(2,1)S(1)}, bf16[3,1,160,384]{3,2,1,0:T(8,128)(2,1)S(1)}, u32[]{:S(2)}, u32[]{:S(2)}) collective-permute-start(bf16[3,1,160,384]{3,2,1,0:T(8,128)(2,1)S(1)} %get-tuple-element.41), channel_id=1, source_target_pairs={{0,4},{4,8},{8,12},{1,5},{5,9},{9,13},{2,6},{6,10},{10,14},{3,7},{... | collective-permute-start | bytes 1105928 | tf_op jit(solution)/shard_map/ppermute | solution.py:20
  31.3 5.3 %collective-permute-start.3 = (bf16[3,1,160,384]{3,2,1,0:T(8,128)(2,1)S(1)}, bf16[3,1,160,384]{3,2,1,0:T(8,128)(2,1)S(1)}, u32[]{:S(2)}, u32[]{:S(2)}) collective-permute-start(bf16[3,1,160,384]{3,2,1,0:T(8,128)(2,1)S(1)} %get-tuple-element.40), channel_id=1, source_target_pairs={{4,0},{8,4},{12,8},{5,1},{9,5},{13,9},{6,2},{10,6},{14,10},{7,3},{... | collective-permute-start | bytes 1105928 | tf_op jit(solution)/shard_map/ppermute | solution.py:21
  47.6 1.0 copy-start.2
  47.6 1.0 copy-start.3
  47.6 1.2 %copy-start.4 = (f32[384]{0:T(512)S(1)}, f32[384]{0:T(512)}, u32[]{:S(2)}) copy-start(f32[384]{0:T(512)} %param.22) | copy-start | bytes 4612
  47.6 1.2 %copy-start.5 = (f32[384]{0:T(512)S(1)}, f32[384]{0:T(512)}, u32[]{:S(2)}) copy-start(f32[384]{0:T(512)} %param.21) | copy-start | bytes 4612
  48.4 1.4 %copy-start.7 = (bf16[384,384]{1,0:T(8,128)(2,1)S(1)}, bf16[384,384]{1,0:T(8,128)(2,1)}, u32[]{:S(2)}) copy-start(bf16[384,384]{1,0:T(8,128)(2,1)} %param.23) | copy-start | bytes 884740
  48.4 1.4 %copy-start.10 = (f32[384]{0:T(512)S(1)}, f32[384]{0:T(512)}, u32[]{:S(2)}) copy-start(f32[384]{0:T(512)} %param.24) | copy-start | bytes 4612
  83.3 5.4 %copy-start.6 = (bf16[1,12,160,384]{3,2,0,1:T(8,128)(2,1)S(1)}, bf16[1,12,160,384]{3,2,0,1:T(8,128)(2,1)}, u32[]{:S(2)}) copy-start(bf16[1,12,160,384]{3,2,0,1:T(8,128)(2,1)} %all-gather.2.cloned.1.call-done) | copy-start | bytes 4423684
  83.3 5.4 %copy-start.8 = (bf16[384,384]{1,0:T(8,128)(2,1)S(1)}, bf16[384,384]{1,0:T(8,128)(2,1)}, u32[]{:S(2)}) copy-start(bf16[384,384]{1,0:T(8,128)(2,1)} %param.26) | copy-start | bytes 884740
  83.3 5.4 %copy-start.11 = (f32[384]{0:T(512)S(1)}, f32[384]{0:T(512)}, u32[]{:S(2)}) copy-start(f32[384]{0:T(512)} %param.27) | copy-start | bytes 4612
  88.7 2.2 %copy-start.1 = (f32[480,1920]{1,0:T(8,128)S(1)}, f32[480,1920]{1,0:T(8,128)}, u32[]{:S(2)}) copy-start(f32[480,1920]{1,0:T(8,128)} %get-tuple-element.43) | copy-start | bytes 11059204
  90.9 1.0 copy-start.9
  90.9 1.0 copy-start.12
  90.9 1.5 %copy-start.13 = (bf16[1920,384]{1,0:T(8,128)(2,1)S(1)}, bf16[1920,384]{1,0:T(8,128)(2,1)}, u32[]{:S(2)}) copy-start(bf16[1920,384]{1,0:T(8,128)(2,1)} %fusion.3) | copy-start | bytes 4423684
Sparse Core Ops, SparseCore 0:
  49.9 33.4 all-gather.1
where the time goes:
time: 104 us
  waiting for transfers between devices  43.5 us (42%)
  matrix products  19.3 us (19%)
  between operations  13.7 us (13%)
  starting transfers between devices  12.1 us (12%)
  other arithmetic  9.02 us (9%)
  local copies, waits for them, and re-layouts  6.02 us (6%)
    all_gather x1, waiting for transfers between devices, shards(): lax.all_gather(normed, 'space', axis=1, tiled=True)  32.2 us
    ppermute x2, waiting for transfers between devices, from_behind(): lax.ppermute(value, axis, [(source, source + steps) for source in range(l...  11.2 us
    ppermute x2, starting transfers between devices, from_behind(): lax.ppermute(value, axis, [(source, source + steps) for source in range(l...  9.48 us
    dot_general x9, matrix products, causal_conv(): jnp.dot(joined, kernel, preferred_element_type=jnp.float32)  6.87 us
    dot_general x1, matrix products, absorb(): jnp.einsum('fqc,fkc->fqk', queries, key_rows, preferred_element_type=jnp....  5.34 us
    slice x1, local copies, waits for them, and re-layouts, causal_conv(): kernel = conv_weight[tap_t, tap_y].reshape(3 * channels, channels)  3.94 us
    dot_general x1, matrix products, shards(): jnp.dot(attended, out_weight, preferred_element_type=jnp.float32) + out_bias  3.54 us
    dot_general x1, matrix products, shards(): jnp.dot(source, value_weight, preferred_element_type=jnp.float32)  2.19 us
  transfers between devices with their start and end apart: 5, of which 4 were waited for; matrix products, arithmetic and copies ran while one was open for 5% of the time, Pallas kernels for 0%

commit v1 on v0

--- a/solution.py
+++ b/solution.py
@@ -2,6 +2,22 @@
 import jax.numpy as jnp
 from jax import lax
 from jax.sharding import PartitionSpec as P
+
+
+def gather_around(x, axis, dim):
+    ways, here, step = (lax.axis_size(axis), lax.axis_index(axis), x.shape[dim])
+    lengths = [n * ways if d == dim else n for d, n in enumerate(x.shape)]
+    full = lax.dynamic_update_slice_in_dim(jnp.zeros(lengths, x.dtype), x, here * step, axis=dim)
+    going_up = going_down = x
+    for far in range(1, ways // 2 + 1):
+        going_up = lax.ppermute(going_up, axis, [(d, (d + 1) % ways) for d in range(ways)])
+        full = lax.dynamic_update_slice_in_dim(full, going_up, (here - far) % ways * step, axis=dim)
+        if 2 * far < ways:
+            going_down = lax.ppermute(going_down, axis, [(d, (d - 1) % ways) for d in range(ways)])
+            full = lax.dynamic_update_slice_in_dim(
+                full, going_down, (here + far) % ways * step, axis=dim
+            )
+    return full
 
 
 def from_behind(value, axis, steps):
@@ -97,7 +113,7 @@
         jnp.zeros((frame_count, query_count), jnp.float32),
         jnp.full((frame_count, query_count), -1e30, jnp.float32),
     )
-    source = lax.all_gather(normed, "space", axis=1, tiled=True).reshape(frame_count, -1, channels)
+    source = gather_around(normed, "space", 1).reshape(frame_count, -1, channels)
     key_rows = jnp.dot(source, key_weight, preferred_element_type=jnp.float32).astype(jnp.bfloat16)
     value_rows = (
         jnp.dot(source, value_weight, preferred_element_type=jnp.float32) + value_bias

time: 104 us -> 84.6 us (0.81)
  the two profiles are of different devices: /device:TPU:0 before, /device:TPU:20 now
where the time goes in v1:
time: 84.6 us; the launch traced here: 84.4 us
  waiting for transfers between devices  40 us (47%)
  matrix products  15.7 us (19%)
  starting transfers between devices  12.4 us (15%)
  other arithmetic  10.2 us (12%)
  local copies, waits for them, and re-layouts  5.76 us (7%)
    ppermute x2, waiting for transfers between devices, from_behind(): lax.ppermute(value, axis, [(source, source + steps) for source in range(l...  24.2 us
    ppermute x2, waiting for transfers between devices, gather_around(): lax.ppermute(going_up, axis, [(d, (d + 1) % ways) for d in range(ways)])  14.7 us
    dot_general x9, matrix products, causal_conv(): jnp.dot(joined, kernel, preferred_element_type=jnp.float32)  6.85 us
    ppermute x2, starting transfers between devices, from_behind(): lax.ppermute(value, axis, [(source, source + steps) for source in range(l...  4.78 us
    dot_general x1, matrix products, absorb(): jnp.einsum('fqk,fkc->fqc', weights, value_rows, preferred_element_type=jn...  4.16 us
    slice x1, local copies, waits for them, and re-layouts, causal_conv(): kernel = conv_weight[tap_t, tap_y].reshape(3 * channels, channels)  3.92 us
    dot_general x1, matrix products, absorb(): jnp.einsum('fqc,fkc->fqk', queries, key_rows, preferred_element_type=jnp....  3.89 us
    ppermute x1, starting transfers between devices, padded_2(): after = lax.ppermute(leading, axis, down)  3.64 us
  transfers between devices with their start and end apart: 7, of which 5 were waited for; matrix products, arithmetic and copies ran while one was open for 5% of the time, Pallas kernels for 0%

profile of v1, /device:TPU:20, one launch (start us, length us, event | category | flops | bytes accessed | tf_op | source)
XLA Modules:
  0.0 84.4 jit_solution(10213105879706401952)
XLA Ops:
  0.0 1.2 %fusion.33 = f32[3,160]{1,0:T(4,128)S(1)} fusion(bf16[1,3,160,384]{3,2,1,0:T(8,128)(2,1)} %param.16), kind=kLoop, calls=%fused_computation.72 | loop fusion | flops 552480 | bytes 370560 | tf_op jit(solution)/shard_map/reduce_sum | solution.py:43
  1.2 1.3 %fusion.41 = bf16[1,3,160,384]{3,2,1,0:T(8,128)(2,1)S(1)} fusion(bf16[1,3,160,384]{3,2,1,0:T(8,128)(2,1)} %param.16, f32[384]{0:T(512)} %param.18, f32[384]{0:T(512)} %param.17, f32[3,160]{1,0:T(4,128)S(1)} %add_rsqrt_fusion.1), kind=kLoop, calls=%fused_computation.80 | loop fusion | flops 1658880 | bytes 742272 | tf_op jit(solution)/shard_map/convert_element_type | solution.py:96
  2.6 1.3 %collective-permute-start = (bf16[1,3,160,384]{3,2,1,0:T(8,128)(2,1)S(1)}, bf16[1,3,160,384]{3,2,1,0:T(8,128)(2,1)S(1)}, u32[]{:S(2)}, u32[]{:S(2)}) collective-permute-start(bf16[1,3,160,384]{3,2,1,0:T(8,128)(2,1)S(1)} %fusion.41), channel_id=1, source_target_pairs={{0,2},{1,3},{4,6},{5,7},{8,10},{9,11},{12,14},{13,15},{16,18},{17,... | collective-permute-start | bytes 1105928 | tf_op jit(solution)/shard_map/ppermute | solution.py:26
  3.9 3.5 %collective-permute-start.1 = (bf16[1,3,160,384]{3,2,1,0:T(8,128)(2,1)S(1)}, bf16[1,3,160,384]{3,2,1,0:T(8,128)(2,1)S(1)}, u32[]{:S(2)}, u32[]{:S(2)}) collective-permute-start(bf16[1,3,160,384]{3,2,1,0:T(8,128)(2,1)S(1)} %fusion.41), channel_id=1, source_target_pairs={{0,1},{1,2},{2,3},{4,5},{5,6},{6,7},{8,9},{9,10},{10,11},{12,13},{... | collective-permute-start | bytes 1105928 | tf_op jit(solution)/shard_map/ppermute | solution.py:26
  7.4 9.5 %collective-permute-done = bf16[1,3,160,384]{3,2,1,0:T(8,128)(2,1)S(1)} collective-permute-done((bf16[1,3,160,384]{3,2,1,0:T(8,128)(2,1)S(1)}, bf16[1,3,160,384]{3,2,1,0:T(8,128)(2,1)S(1)}, u32[]{:S(2)}, u32[]{:S(2)}) %collective-permute-start) | collective-permute-done | bytes 368672 | tf_op jit(solution)/shard_map/ppermute | solution.py:26
  16.9 14.7 %collective-permute-done.1 = bf16[1,3,160,384]{3,2,1,0:T(8,128)(2,1)S(1)} collective-permute-done((bf16[1,3,160,384]{3,2,1,0:T(8,128)(2,1)S(1)}, bf16[1,3,160,384]{3,2,1,0:T(8,128)(2,1)S(1)}, u32[]{:S(2)}, u32[]{:S(2)}) %collective-permute-start.1) | collective-permute-done | bytes 368672 | tf_op jit(solution)/shard_map/ppermute | solution.py:26
  31.5 0.1 pad_maximum_fusion.21
  31.6 1.9 %collective-permute-start.2 = (bf16[3,1,160,384]{3,2,1,0:T(8,128)(2,1)S(1)}, bf16[3,1,160,384]{3,2,1,0:T(8,128)(2,1)S(1)}, u32[]{:S(2)}, u32[]{:S(2)}) collective-permute-start(bf16[3,1,160,384]{3,2,1,0:T(8,128)(2,1)S(1)} %get-tuple-element.43), channel_id=1, source_target_pairs={{0,4},{4,8},{8,12},{1,5},{5,9},{9,13},{2,6},{6,10},{10,14},{3,7},{... | collective-permute-start | bytes 1105928 | tf_op jit(solution)/shard_map/ppermute | solution.py:36
  33.6 3.6 %collective-permute-start.3 = (bf16[3,1,160,384]{3,2,1,0:T(8,128)(2,1)S(1)}, bf16[3,1,160,384]{3,2,1,0:T(8,128)(2,1)S(1)}, u32[]{:S(2)}, u32[]{:S(2)}) collective-permute-start(bf16[3,1,160,384]{3,2,1,0:T(8,128)(2,1)S(1)} %get-tuple-element.42), channel_id=1, source_target_pairs={{4,0},{8,4},{12,8},{5,1},{9,5},{13,9},{6,2},{10,6},{14,10},{7,3},{... | collective-permute-start | bytes 1105928 | tf_op jit(solution)/shard_map/ppermute | solution.py:37
  37.2 3.9 %fusion.49 = (bf16[1,1,3,384,384]{4,3,2,1,0:T(8,128)(2,1)S(1)}, bf16[1,1,3,384,384]{4,3,2,1,0:T(8,128)(2,1)S(1)}, bf16[1,1,3,384,384]{4,3,2,1,0:T(8,128)(2,1)S(1...) fusion(bf16[3,3,3,384,384]{4,3,2,1,0:T(8,128)(2,1)} %param.19), kind=kLoop, calls=%fused_computation.98 | loop fusion | bytes 15925248 | tf_op jit(solution)/shard_map/slice | solution.py:57
  41.1 1.1 %collective-permute-done.3 = bf16[3,1,160,384]{3,2,1,0:T(8,128)(2,1)S(1)} collective-permute-done((bf16[3,1,160,384]{3,2,1,0:T(8,128)(2,1)S(1)}, bf16[3,1,160,384]{3,2,1,0:T(8,128)(2,1)S(1)}, u32[]{:S(2)}, u32[]{:S(2)}) %collective-permute-start.3) | collective-permute-done | bytes 368672 | tf_op jit(solution)/shard_map/ppermute | solution.py:37
  42.2 1.5 %select_maximum_fusion = bf16[3,5,162,384]{3,2,1,0:T(8,128)(2,1)S(1)} fusion(bf16[3,1,160,384]{3,2,1,0:T(8,128)(2,1)S(1)} %collective-permute-done.3, bf16[3,1,160,384]{3,2,1,0:T(8,128)(2,1)S(1)} %collective-permute-done.2, bf16[1,3,160,384]{3,2,1,0:T(8,128)(2,1)S(1)} %fusion.41, bf16[1,3,160,384]{3,2,1,0:T(8,128)(2,1)S(1)} %collective-permute-done.1, ...), kind=kLoop, calls=%fused_computation.10 | loop fusion | flops 16796160 | bytes 3709440 | tf_op jit(solution)/shard_map/concatenate | solution.py:38
  43.8 1.1 %fusion.50 = (bf16[1,3,160,384]{3,2,1,0:T(8,128)(2,1)S(1)}, bf16[1,3,160,384]{3,2,1,0:T(8,128)(2,1)S(1)}, bf16[1,3,160,384]{3,2,1,0:T(8,128)(2,1)S(1)}, bf16[1,3...) fusion(bf16[3,5,162,384]{3,2,1,0:T(8,128)(2,1)S(1)} %select_max, ...), kind=kLoop, calls=%fused_computation.99 | loop fusion | bytes 13271040 | tf_op jit(solution)/shard_map/slice | solution.py:54
  44.9 1.3 %fusion.18 = (bf16[1,3,160,1152]{3,2,1,0:T(8,128)(2,1)S(1)}, bf16[1,3,160,1152]{3,2,1,0:T(8,128)(2,1)S(1)}, bf16[1,3,160,1152]{3,2,1,0:T(8,128)(2,1)S(1)}) fusion(bf16[3,1,160,384]{3,2,1,0:T(8,128)(2,1)S(1)} %collective-permute-done.2, bf16[1,3,160,384]{3,2,1,0:T(8,128)(2,1)S(1)} %fusion.41, bf16[1,3,160,384]{3,2,1,0:T(8,128)(2,1)S(1)} %collective-permute-done.1, ...), kind=kLoop, calls=%fused_computation.39 | loop fusion | flops 19906560 | bytes 7004160 | tf_op jit(solution)/shard_map/concatenate | solution.py:53
  46.2 0.8 fusion.51
  47.0 0.1 pad_maximum_fusion.20
  47.1 0.2 pad_maximum_fusion.18
  47.3 0.8 convolution_add_fusion.10
  48.1 0.4 fusion.16
  48.4 0.8 convolution_add_fusion.9
  49.2 0.8 convolution_add_fusion.8
  50.0 0.8 convolution_add_fusion.7
  50.7 0.8 convolution_add_fusion.6
  51.5 0.8 convolution_add_fusion.5
  52.3 0.8 convolution_add_fusion.4
  53.1 0.0 copy-start.1
  53.1 0.8 convolution_add_fusion.3
  53.9 0.0 copy-start.5
  53.9 0.2 copy-done.1
  54.0 0.2 fusion.42
  54.3 0.1 broadcast_in_dim.4
  54.4 0.1 copy-done.4
  54.6 0.0 copy-done.5
  54.6 0.2 constant_dynamic-update-slice_fusion.3
  54.8 0.1 collective-permute-start.4
  54.9 2.0 %collective-permute-start.5 = (bf16[1,3,160,384]{3,2,1,0:T(8,128)(2,1)S(1)}, bf16[1,3,160,384]{3,2,1,0:T(8,128)(2,1)S(1)}, u32[]{:S(2)}, u32[]{:S(2)}) collective-permute-start(bf16[1,3,160,384]{3,2,1,0:T(8,128)(2,1)S(1)} %get-tuple-element.6), channel_id=1, source_target_pairs={{0,12},{4,0},{8,4},{12,8},{1,13},{5,1},{9,5},{13,9},{2,14},{6,2},{... | collective-permute-start | bytes 1105928 | tf_op jit(solution)/shard_map/ppermute | solution.py:16
  56.9 8.3 %collective-permute-done.4 = bf16[1,3,160,384]{3,2,1,0:T(8,128)(2,1)S(1)} collective-permute-done((bf16[1,3,160,384]{3,2,1,0:T(8,128)(2,1)S(1)}, bf16[1,3,160,384]{3,2,1,0:T(8,128)(2,1)S(1)}, u32[]{:S(2)}, u32[]{:S(2)}) %collective-permute-start.4) | collective-permute-done | bytes 368672 | tf_op jit(solution)/shard_map/ppermute | solution.py:13
  65.2 0.4 fusion.14
  65.6 0.1 constant_dynamic-update-slice_fusion.2
  65.7 0.1 constant_dynamic-update-slice_fusion.1
  65.8 6.4 %collective-permute-done.6 = bf16[1,3,160,384]{3,2,1,0:T(8,128)(2,1)S(1)} collective-permute-done((bf16[1,3,160,384]{3,2,1,0:T(8,128)(2,1)S(1)}, bf16[1,3,160,384]{3,2,1,0:T(8,128)(2,1)S(1)}, u32[]{:S(2)}, u32[]{:S(2)}) %collective-permute-start.6) | collective-permute-done | bytes 368672 | tf_op jit(solution)/shard_map/ppermute | solution.py:13
  72.2 0.1 constant_dynamic-update-slice_fusion
  72.2 3.9 %multiply_reduce_fusion = (f32[480]{0:T(512)S(1)}, f32[480,1920]{1,0:T(8,128)}) fusion(bf16[480,384]{1,0:T(8,128)(2,1)S(1)} %fusion.14, bf16[1920,384]{1,0:T(8,128)(2,1)S(1)} %bitcast.67, bf16[384,384]{1,0:T(8,128)(2,1)S(1)} %copy-done), kind=kOutput, calls=%fused_computation.4 | convolution fusion | flops 1276599808 | bytes 5826432 | tf_op jit(solution)/shard_map/fqc,fkc->fqk/dot_general | solution.py:65
  76.1 2.8 %fusion.1 = f32[480]{0:T(512)S(1)} fusion(f32[480,1920]{1,0:T(8,128)} %get-tuple-element.45, f32[480]{0:T(512)S(1)} %broadcast_maximum_fusion), kind=kLoop, calls=%fused_computation.5 | loop fusion | flops 2764320 | bytes 3690240 | tf_op jit(solution)/shard_map/reduce_sum | solution.py:73
  79.0 0.0 copy-start.6
  79.0 4.2 %fusion.30 = bf16[480,384]{1,0:T(8,128)(2,1)S(1)} fusion(bf16[1920,384]{1,0:T(8,128)(2,1)S(1)} %bitcast.68, bf16[384,384]{1,0:T(8,128)(2,1)S(1)} %copy-done.8, f32[384]{0:T(512)S(1)} %copy-done.10, f32[480,1920]{1,0:T(8,128)} %get-tuple-element.45, f32[480]{0:T(512)S(1)} %broadcast_maximum_fusion, f32[480]{0:T(512)S(1)} %fusion.1), kind=kOutput, calls=%fused_computation.69 | convolution fusion | flops 1278627840 | bytes 5829888 | tf_op jit(solution)/shard_map/fqk,fkc->fqc/dot_general | solution.py:71
  83.2 0.4 convolution_add_fusion.1
  83.6 0.8 fusion.46
  (22 shorter events, 0.1 us)
Async XLA Ops:
  0.0 72.2 %copy-start = (bf16[384,384]{1,0:T(8,128)(2,1)S(1)}, bf16[384,384]{1,0:T(8,128)(2,1)}, u32[]{:S(2)}) copy-start(bf16[384,384]{1,0:T(8,128)(2,1)} %param.25) | copy-start | bytes 884740
  2.6 14.3 %collective-permute-start = (bf16[1,3,160,384]{3,2,1,0:T(8,128)(2,1)S(1)}, bf16[1,3,160,384]{3,2,1,0:T(8,128)(2,1)S(1)}, u32[]{:S(2)}, u32[]{:S(2)}) collective-permute-start(bf16[1,3,160,384]{3,2,1,0:T(8,128)(2,1)S(1)} %fusion.41), channel_id=1, source_target_pairs={{0,2},{1,3},{4,6},{5,7},{8,10},{9,11},{12,14},{13,15},{16,18},{17,... | collective-permute-start | bytes 1105928 | tf_op jit(solution)/shard_map/ppermute | solution.py:26
  3.9 27.7 %collective-permute-start.1 = (bf16[1,3,160,384]{3,2,1,0:T(8,128)(2,1)S(1)}, bf16[1,3,160,384]{3,2,1,0:T(8,128)(2,1)S(1)}, u32[]{:S(2)}, u32[]{:S(2)}) collective-permute-start(bf16[1,3,160,384]{3,2,1,0:T(8,128)(2,1)S(1)} %fusion.41), channel_id=1, source_target_pairs={{0,1},{1,2},{2,3},{4,5},{5,6},{6,7},{8,9},{9,10},{10,11},{12,13},{... | collective-permute-start | bytes 1105928 | tf_op jit(solution)/shard_map/ppermute | solution.py:26
  31.6 9.5 %collective-permute-start.2 = (bf16[3,1,160,384]{3,2,1,0:T(8,128)(2,1)S(1)}, bf16[3,1,160,384]{3,2,1,0:T(8,128)(2,1)S(1)}, u32[]{:S(2)}, u32[]{:S(2)}) collective-permute-start(bf16[3,1,160,384]{3,2,1,0:T(8,128)(2,1)S(1)} %get-tuple-element.43), channel_id=1, source_target_pairs={{0,4},{4,8},{8,12},{1,5},{5,9},{9,13},{2,6},{6,10},{10,14},{3,7},{... | collective-permute-start | bytes 1105928 | tf_op jit(solution)/shard_map/ppermute | solution.py:36
  33.6 8.7 %collective-permute-start.3 = (bf16[3,1,160,384]{3,2,1,0:T(8,128)(2,1)S(1)}, bf16[3,1,160,384]{3,2,1,0:T(8,128)(2,1)S(1)}, u32[]{:S(2)}, u32[]{:S(2)}) collective-permute-start(bf16[3,1,160,384]{3,2,1,0:T(8,128)(2,1)S(1)} %get-tuple-element.42), channel_id=1, source_target_pairs={{4,0},{8,4},{12,8},{5,1},{9,5},{13,9},{6,2},{10,6},{14,10},{7,3},{... | collective-permute-start | bytes 1105928 | tf_op jit(solution)/shard_map/ppermute | solution.py:37
  53.1 1.0 %copy-start.1 = (bf16[1,3,160,384]{3,2,1,0:T(8,128)(2,1)S(1)}, bf16[1,3,160,384]{3,2,1,0:T(8,128)(2,1)}, u32[]{:S(2)}) copy-start(bf16[1,3,160,384]{3,2,1,0:T(8,128)(2,1)} %param.15) | copy-start | bytes 1105924
  53.1 1.0 %copy-start.3 = (f32[384]{0:T(512)S(1)}, f32[384]{0:T(512)}, u32[]{:S(2)}) copy-start(f32[384]{0:T(512)} %param.20) | copy-start | bytes 4612
  53.9 0.7 copy-start.4
  53.9 0.7 copy-start.5
  54.0 11.2 %copy-start.7 = (bf16[384,384]{1,0:T(8,128)(2,1)S(1)}, bf16[384,384]{1,0:T(8,128)(2,1)}, u32[]{:S(2)}) copy-start(bf16[384,384]{1,0:T(8,128)(2,1)} %param.23) | copy-start | bytes 884740
  54.0 11.2 %copy-start.9 = (f32[384]{0:T(512)S(1)}, f32[384]{0:T(512)}, u32[]{:S(2)}) copy-start(f32[384]{0:T(512)} %param.24) | copy-start | bytes 4612
  54.8 10.4 %collective-permute-start.4 = (bf16[1,3,160,384]{3,2,1,0:T(8,128)(2,1)S(1)}, bf16[1,3,160,384]{3,2,1,0:T(8,128)(2,1)S(1)}, u32[]{:S(2)}, u32[]{:S(2)}) collective-permute-start(bf16[1,3,160,384]{3,2,1,0:T(8,128)(2,1)S(1)} %get-tuple-element.6), channel_id=1, source_target_pairs={{0,4},{4,8},{8,12},{12,0},{1,5},{5,9},{9,13},{13,1},{2,6},{6,10},{... | collective-permute-start | bytes 1105928 | tf_op jit(solution)/shard_map/ppermute | solution.py:13
  54.9 10.8 %collective-permute-start.5 = (bf16[1,3,160,384]{3,2,1,0:T(8,128)(2,1)S(1)}, bf16[1,3,160,384]{3,2,1,0:T(8,128)(2,1)S(1)}, u32[]{:S(2)}, u32[]{:S(2)}) collective-permute-start(bf16[1,3,160,384]{3,2,1,0:T(8,128)(2,1)S(1)} %get-tuple-element.6), channel_id=1, source_target_pairs={{0,12},{4,0},{8,4},{12,8},{1,13},{5,1},{9,5},{13,9},{2,14},{6,2},{... | collective-permute-start | bytes 1105928 | tf_op jit(solution)/shard_map/ppermute | solution.py:16
  65.2 6.9 %collective-permute-start.6 = (bf16[1,3,160,384]{3,2,1,0:T(8,128)(2,1)S(1)}, bf16[1,3,160,384]{3,2,1,0:T(8,128)(2,1)S(1)}, u32[]{:S(2)}, u32[]{:S(2)}) collective-permute-start(bf16[1,3,160,384]{3,2,1,0:T(8,128)(2,1)S(1)} %collective-permute-done.4), channel_id=1, source_target_pairs={{0,4},{4,8},{8,12},{12,0},{1,5},{5,9},{9,13},{13,1},{2,6},{6,10},{... | collective-permute-start | bytes 1105928 | tf_op jit(solution)/shard_map/ppermute | solution.py:13
  76.1 2.8 %copy-start.8 = (bf16[384,384]{1,0:T(8,128)(2,1)S(1)}, bf16[384,384]{1,0:T(8,128)(2,1)}, u32[]{:S(2)}) copy-start(bf16[384,384]{1,0:T(8,128)(2,1)} %param.26) | copy-start | bytes 884740
  76.1 2.8 %copy-start.10 = (f32[384]{0:T(512)S(1)}, f32[384]{0:T(512)}, u32[]{:S(2)}) copy-start(f32[384]{0:T(512)} %param.27) | copy-start | bytes 4612
  79.0 4.2 %copy-start.2 = (bf16[384,384]{1,0:T(8,128)(2,1)S(1)}, bf16[384,384]{1,0:T(8,128)(2,1)}, u32[]{:S(2)}) copy-start(bf16[384,384]{1,0:T(8,128)(2,1)} %param.28) | copy-start | bytes 884740
  79.0 4.2 %copy-start.6 = (f32[384]{0:T(512)S(1)}, f32[384]{0:T(512)}, u32[]{:S(2)}) copy-start(f32[384]{0:T(512)} %param.29) | copy-start | bytes 4612
